TPU v7x, 128 devices: a whole 4x4x4 slice. The times are simulated.
128 devices in a mesh: wake: 16 (over y_hi, x, core), grid: 8 (over z, y_lo).
Axes of the slice: x: 4, y: 4 (y_hi: 2, y_lo: 2; y = y_hi * 2 + y_lo), z: 4, core: 2. Of those that a mesh axis runs over, the one named last changes fastest.
Arguments:
- flow: float32 [5, 256, 131072], P(None, 'wake', 'grid'), may hold values from -6 to 6
- section_map: int32 [256, 131072], P('wake', 'grid'), may hold values from 0 to 2
- viscosity: float32 [3, 5], replicated, may hold values from 0.12 to 0.24
- particle_position: float32 [3, 32768], P(None, ('wake', 'grid')), may hold values from 0 to 1
- particle_strength: float32 [3, 32768], P(None, ('wake', 'grid')), may hold values from -0.6 to 0.6
- particle_core: float32 [32768], P(('wake', 'grid')), may hold values from 0.08 to 0.16
- shed_counts: int32 [16], replicated, may hold values from 512 to 2048, as said below
- node_position: float32 [3, 131072], P(None, ('wake', 'grid')), may hold values from 0 to 1
- node_block: int32 [131072, 1], P(('wake', 'grid')), may hold values from 0 to 15; in each aligned block of 1024 rows (0 to 1023, 1024 to 2047, ...) at most 128 rows name the same one
Outputs:
- flow_out: float32 [5, 256, 131072], P(None, 'wake', 'grid')
- particle_velocity: float32 [3, 32768], P(None, ('wake', 'grid'))
- particle_stretching: float32 [3, 32768], P(None, ('wake', 'grid'))
Inputs may be any that keep to these rules, and one draw needn't show every extreme that they name: `shed_counts`: at least one block holds 2048 live particles. `node_block`: among the 1024 nodes of one device (aligned blocks of nodes), at most 128 name any one block, and some block is named by exactly 128.
All inputs are finite; a program needn't handle non-finite values.
Results may differ from a plain program's by a relative error of at most 0.0003.
Values sent between devices are 32-bit elements; how exact they have to be, the bound alone decides.
A program may use at most 192 MiB of HBM per device.

v0:
```python
import math
import jax
import jax.numpy as jnp
from jax import lax
from jax.sharding import PartitionSpec as P

NSEC = 3
NODE_Z = 64
PB = 2048
SWEEPS = 3
inverse_four_pi = 1.0 / (4.0 * math.pi)


def from_behind(value, axis, by):
    count = lax.axis_size(axis)
    return lax.ppermute(value, axis, [(i, (i + by) % count) for i in range(count)])


def extended(cells, sides, width):
    for axis, dim in sides:
        count = lax.axis_size(axis)
        ends = count - 1
        head = lax.slice_in_dim(cells, 0, width, axis=dim)
        tail = lax.slice_in_dim(cells, cells.shape[dim] - width, cells.shape[dim], axis=dim)
        cells = jnp.concatenate(
            [
                lax.ppermute(tail, axis, [(i, (i + 1) % count) for i in range(ends)]),
                cells,
                lax.ppermute(head, axis, [((i + 1) % count, i) for i in range(ends)]),
            ],
            axis=dim,
        )
    return cells


def cross_three(first, second):
    return (
        first[1] * second[2] - first[2] * second[1],
        first[2] * second[0] - first[0] * second[2],
        first[0] * second[1] - first[1] * second[0],
    )


def particle_rates(place, spin, core, live, source, source_live):
    delta = [place[component][:, None] - source[component][None, :] for component in range(3)]
    spread = 0.5 * (core[:, None] * core[:, None] + source[6][None, :] * source[6][None, :])
    distance = delta[0] * delta[0] + delta[1] * delta[1] + delta[2] * delta[2] + spread
    weight = jnp.where(source_live[None, :], distance ** (-1.5), 0.0)
    steep = 3.0 * weight / distance
    source_spin = [source[3 + component][None, :] for component in range(3)]
    curl = cross_three(delta, source_spin)
    along = spin[0][:, None] * delta[0] + spin[1][:, None] * delta[1] + spin[2][:, None] * delta[2]
    velocity = jnp.stack([jnp.sum(weight * curl[component], axis=1) for component in range(3)])
    spin_sum = [jnp.sum(weight * source_spin[component], axis=1) for component in range(3)]
    bent = jnp.stack([jnp.sum(steep * along * curl[component], axis=1) for component in range(3)])
    turned = jnp.stack(cross_three(spin, spin_sum))
    factor = jnp.where(live, -inverse_four_pi, 0.0)[None, :]
    return (velocity * factor, (turned - bent) * factor)


def node_rates(points, source, source_live):
    delta = [points[component][:, None] - source[component][None, :] for component in range(3)]
    distance = (
        delta[0] * delta[0]
        + delta[1] * delta[1]
        + delta[2] * delta[2]
        + source[6][None, :] * source[6][None, :]
    )
    weight = jnp.where(source_live[None, :], distance ** (-1.5), 0.0)
    source_spin = [source[3 + component][None, :] for component in range(3)]
    curl = cross_three(delta, source_spin)
    return (
        jnp.stack([jnp.sum(weight * curl[component], axis=1) for component in range(3)])
        * -inverse_four_pi
    )


def tiled(function, arrays, count):
    tile = math.gcd(count, 256)
    pieces = count // tile

    def split_tiles(array):
        return jnp.moveaxis(array.reshape(array.shape[:-1] + (pieces, tile)), -2, 0)

    def join_tiles(array):
        moved = jnp.moveaxis(array, 0, -2)
        return moved.reshape(moved.shape[:-2] + (count,))

    results = lax.map(function, tuple((split_tiles(array) for array in arrays)))
    return jax.tree.map(join_tiles, results)


def cell_diffusion(sections, viscosity):
    total = jnp.zeros((5,) + sections.shape, jnp.float32)
    for number in range(NSEC):
        total = total + jnp.where(sections[None] == number, viscosity[number][:, None, None], 0.0)
    return total


def on_device(
    flow,
    section_map,
    viscosity,
    particle_position,
    particle_strength,
    particle_core,
    shed_counts,
    node_position,
    node_block,
):
    wake_count = lax.axis_size("wake")
    wake_index = lax.axis_index("wake")
    stops = wake_count // 2
    half = stops // 2
    slots = jnp.arange(PB, dtype=jnp.int32)
    target_count = particle_position.shape[1]
    target_slots = lax.axis_index("grid") * target_count + jnp.arange(target_count, dtype=jnp.int32)
    target_live = target_slots < shed_counts[wake_index]
    share = jnp.concatenate([particle_position, particle_strength, particle_core[None, :]], axis=0)
    block = lax.all_gather(share, "grid", axis=1, tiled=True)

    def visit(source, number, totals):
        source_live = slots < shed_counts[number]

        def visit_rates(arrays):
            return particle_rates(arrays[0], arrays[1], arrays[2], arrays[3], source, source_live)

        velocity, stretch = tiled(
            visit_rates,
            (particle_position, particle_strength, particle_core, target_live),
            target_count,
        )
        return (totals[0] + velocity, totals[1] + stretch)

    zeros = jnp.zeros((3, target_count), jnp.float32)
    first = from_behind(block, "wake", 1 - half)
    totals = visit(first, (wake_index + half - 1) % wake_count, (zeros, zeros))

    def advance(turn, carry):
        source, sums = carry
        source = from_behind(source, "wake", 1)
        return (source, visit(source, (wake_index + half - 1 - turn) % wake_count, sums))

    carried, totals = lax.fori_loop(1, stops, advance, (first, totals))
    node_count = node_position.shape[1]
    target_block = node_block[:, 0]
    capacity = 2 * node_count // wake_count
    onehot = (target_block[:, None] == jnp.arange(wake_count, dtype=jnp.int32)[None, :]).astype(
        jnp.int32
    )
    rank = jnp.sum((jnp.cumsum(onehot, axis=0) - onehot) * onehot, axis=1)
    slot = target_block * capacity + rank
    outgoing = jnp.zeros((3, wake_count * capacity), jnp.float32).at[:, slot].set(node_position)
    outgoing = outgoing.reshape(3, wake_count, capacity)
    own_live = slots < shed_counts[wake_index]
    points = lax.all_to_all(outgoing, "wake", split_axis=1, concat_axis=1, tiled=True)
    flat = points.reshape(3, -1)

    def evaluate_rates(arrays):
        return node_rates(arrays[0], block, own_live)

    result = tiled(evaluate_rates, (flat,), flat.shape[1])
    answered = result.reshape(points.shape)
    returned = lax.all_to_all(answered, "wake", split_axis=1, concat_axis=1, tiled=True)
    node_velocity = returned.reshape(3, wake_count * capacity)[:, slot]
    rows = flow.shape[1]
    columns = flow.shape[2]
    stride = columns // NODE_Z
    field = flow.at[1:4, :, ::stride].set(node_velocity.reshape(3, rows, NODE_Z))
    diffusion = cell_diffusion(section_map, viscosity)
    for sweep in range(SWEEPS):
        padded = extended(field, (("wake", 1), ("grid", 2)), 1)
        beside = (
            padded[:, 2:, 1:-1] + padded[:, :-2, 1:-1] + padded[:, 1:-1, 2:] + padded[:, 1:-1, :-2]
        )
        field = field + diffusion * (beside - 4.0 * field)
    return (field, totals[0], totals[1])


def solution(mesh):
    return jax.shard_map(
        on_device,
        mesh=mesh,
        in_specs=(
            P(None, "wake", "grid"),
            P("wake", "grid"),
            P(),
            P(None, ("wake", "grid")),
            P(None, ("wake", "grid")),
            P(("wake", "grid")),
            P(),
            P(None, ("wake", "grid")),
            P(("wake", "grid"), None),
        ),
        out_specs=(P(None, "wake", "grid"), P(None, ("wake", "grid")), P(None, ("wake", "grid"))),
        check_vma=False,
    )
```

profile of v0, /device:TPU:80, one launch (start us, length us, event | category | flops | bytes accessed | tf_op | source)
XLA Modules:
  0.0 859.3 jit_solution(195151444402644081)
XLA Ops:
  13.0 7.3 all-to-all-start
  20.4 27.0 %all_gather.3 = f32[7,2048]{1,0:T(8,128)} all-gather(f32[7,256]{1,0:T(8,128)S(1)} %pad_maximum_fusion.33), channel_id=1, replica_groups=mesh['wake'=16,'grid'=8] {'grid'}, dimensions={1}, use_global_device_ids=true | all-gather | bytes 64512 | tf_op jit(solution)/shard_map/all_gather | solution.py:120
  49.3 42.7 %while.50 = (s32[]{:T(128)}, f32[8,3,256]{2,1,0:T(4,128)}, f32[8,3,256]{2,0,1:T(8,128)S(1)}, f32[7,2048]{1,0:T(8,128)}, f32[1,2048]{1,0:T(1,128)S(1)}, /*index=5*/s32[]{:T(128)}, s32[]{:T(128)}, s32[]{:T(128)}, s32[]{}, s32[]{}) while((s32[]{:T(128)}, f32[8,3,256]{2,1,0:T(4,128)}, f32[8,3,256]{2,0,1:T(8,128)S(1)}, ...), condition=%wide.region_8.9_spmd.clone, body=%wide.region_4.8_spmd.clone.sunk | while | flops 13110788 | bytes 179853 | solution.py:89
  92.1 7.5 all-to-all-start.1
  99.6 20.3 %copy.69 = f32[5,16,16384]{1,2,0:T(8,128)} copy(f32[5,16,16384]{2,1,0:T(8,128)} %param.13) | data formatting | bytes 10485760
  123.6 489.6 %while.49 = (s32[]{:T(128)}, f32[5,16,16384]{1,2,0:T(8,128)}, s32[64,2]{0,1:T(2,128)S(1)}, f32[64,3,16]{2,0,1:T(8,128)S(1)}, s32[]{:T(128)}, /*index=5*/s32[3]{0:T(128)S(1)}, s32[1]{0:T(128)}, s32[]{:T(128)}) while((s32[]{:T(128)}, f32[5,16,16384]{1,2,0:T(8,128)}, s32[64,2]{0,1:T(2,128)S(1)}, f32[64,3,16]{2,0,1:T(8,128)S(1)}, s32[]{:T(128)}, ...), condition=%wide.while_cond, body=%wide.while_body.sunk | while | flops 67 | bytes 1123 | solution.py:169
  613.2 27.6 %copy.76 = f32[5,16,16384]{2,0,1:T(8,128)} copy(f32[5,16,16384]{1,2,0:T(8,128)} %get-tuple-element.407) | data formatting | bytes 10485760 | tf_op jit(solution)/shard_map/scatter | solution.py:169
  653.1 7.5 collective-permute-done.2
  661.6 4.7 collective-permute-start.3
  673.5 17.5 %fusion.60 = f32[5,16,16384]{2,0,1:T(8,128)S(1)} fusion(f32[5,16,16384]{2,0,1:T(8,128)} %copy.76, f32[5,18,1]{2,0,1:T(8,128)S(1)} %collective-permute-done.4, f32[5,1,16384]{2,0,1:T(8,128)S(1)} %collective-permute-done.1, f32[5,1,16384]{2,0,1:T(8,128)S(1)} %collective-permute-done.2, f32[5,18,1]{2,0,1:T(8,128)S(1)} %collective-permute-done.3, ...), kind=kLoop, calls=%fused_computation.117 | loop fusion | flops 26214400 | bytes 11928332 | tf_op jit(solution)/shard_map/add | solution.py:176
  699.7 7.5 collective-permute-done.6
  717.6 11.0 %fusion.54 = f32[5,16,16384]{2,0,1:T(8,128)S(1)} fusion(f32[5,16,16384]{2,0,1:T(8,128)S(1)} %fusion.60, f32[5,18,1]{2,0,1:T(8,128)S(1)} %collective-permute-done.8, f32[5,1,16384]{2,0,1:T(8,128)S(1)} %collective-permute-done.5, f32[5,1,16384]{2,0,1:T(8,128)S(1)} %collective-permute-done.6, f32[5,18,1]{2,0,1:T(8,128)S(1)} %collective-permute-done.7, ...), kind=kLoop, calls=%fused_computation.103 | loop fusion | flops 26214400 | bytes 11928332 | tf_op jit(solution)/shard_map/add | solution.py:176
  730.6 7.3 collective-permute-start.9
  737.9 5.0 fusion.79
  750.9 4.8 collective-permute-done.12
  755.7 11.0 %fusion.48 = f32[5,16,16384]{2,0,1:T(8,128)S(1)} fusion(f32[5,16,16384]{2,0,1:T(8,128)S(1)} %fusion.54, f32[5,18,1]{2,0,1:T(8,128)S(1)} %collective-permute-done.12, f32[5,1,16384]{2,0,1:T(8,128)S(1)} %collective-permute-done.9, f32[5,1,16384]{2,0,1:T(8,128)S(1)} %collective-permute-done.10, f32[5,18,1]{2,0,1:T(8,128)S(1)} %collective-permute-done.11, ...), kind=kLoop, calls=%fused_computation.89 | loop fusion | flops 26214400 | bytes 11928332 | tf_op jit(solution)/shard_map/add | solution.py:176
  766.7 5.4 copy.77
  772.1 86.5 %while.51 = (s32[]{:T(128)}, f32[7,2048]{1,0:T(8,128)S(1)}, f32[3,256]{1,0:T(4,128)S(1)}, f32[3,256]{1,0:T(4,128)S(1)}, s32[]{:T(128)}, /*index=5*/s32[16]{0:T(1...) while((s32[]{:T(128)}, f32[7,2048]{1,0:T(8,128)S(1)}, ...), condition=%wide.region_29.30_spmd.clone, body=%wide.region_19.29_spmd.clone.sunk | while | flops 24654864 | bytes 581992 | solution.py:144
  773.9 5.5 collective-permute-done
  779.5 4.9 fusion.117
  786.3 5.5 collective-permute-done
  791.8 4.9 fusion.117
  798.7 5.5 collective-permute-done
  804.2 4.9 fusion.117
  811.1 5.5 collective-permute-done
  816.6 4.9 fusion.117
  823.5 5.5 collective-permute-done
  829.0 4.9 fusion.117
  835.8 5.5 collective-permute-done
  841.3 4.9 fusion.117
  848.2 5.5 collective-permute-done
  853.7 4.9 fusion.117
  (505 shorter events, 613.4 us)
Async XLA Ops:
  0.6 19.7 %copy-start.6 = (f32[256]{0:T(256)S(1)}, f32[256]{0:T(256)}, u32[]{:S(2)}) copy-start(f32[256]{0:T(256)} %param.18) | copy-start | bytes 3076
  0.6 19.7 %copy-start.4 = (f32[3,256]{1,0:T(4,128)S(1)}, f32[3,256]{1,0:T(4,128)}, u32[]{:S(2)}) copy-start(f32[3,256]{1,0:T(4,128)} %param.16) | copy-start | bytes 9220
  0.7 19.7 %copy-start.1 = (f32[3,256]{1,0:T(4,128)S(1)}, f32[3,256]{1,0:T(4,128)}, u32[]{:S(2)}) copy-start(f32[3,256]{1,0:T(4,128)} %param.17) | copy-start | bytes 9220
  0.7 47.6 %copy-start = (s32[16,16384]{1,0:T(8,128)S(1)}, s32[16,16384]{1,0:T(8,128)}, u32[]{:S(2)}) copy-start(s32[16,16384]{1,0:T(8,128)} %param.14) | copy-start | bytes 3145732
  8.7 39.9 %copy-start.8 = (f32[3,5]{1,0:T(4,128)S(1)}, f32[3,5]{1,0:T(4,128)}, u32[]{:S(2)}) copy-start(f32[3,5]{1,0:T(4,128)} %param.15) | copy-start | bytes 184
  8.7 40.0 %copy-start.7 = (s32[16]{0:T(128)S(1)}, s32[16]{0:T(128)}, u32[]{:S(2)}) copy-start(s32[16]{0:T(128)} %param.19) | copy-start | bytes 196
  13.0 36.3 %all-to-all-start = ((f32[3,16,128]{2,0,1:T(4,128)}), f32[3,16,128]{2,0,1:T(4,128)S(1)}, u32[]{:S(2)}, u32[]{:S(2)}) async-start(f32[3,16,128]{2,0,1:T(4,128)} %copy.62), calls=%async_computation | async-start | bytes 65536 | tf_op jit(solution)/shard_map/all_to_all | solution.py:156
  47.3 666.0 %collective-permute-start.13 = (f32[7,2048]{1,0:T(8,128)}, f32[7,2048]{1,0:T(8,128)S(1)}, u32[]{:S(2)}, u32[]{:S(2)}) collective-permute-start(f32[7,2048]{1,0:T(8,128)} %all_gather.3), channel_id=1, source_target_pairs={{0,104},{8,112},{16,120},{24,0},{32,8},{40,16},{48,24},{56,32},{64... | collective-permute-start | bytes 172040 | tf_op jit(solution)/shard_map/ppermute | solution.py:16
  92.1 27.9 %all-to-all-start.1 = ((f32[3,16,128]{2,0,1:T(4,128)}), f32[3,16,128]{2,0,1:T(4,128)S(1)}, u32[]{:S(2)}, u32[]{:S(2)}) async-start(f32[3,16,128]{2,0,1:T(4,128)} %bitcast.12), calls=%async_computation.1 | async-start | bytes 65536 | tf_op jit(solution)/shard_map/all_to_all | solution.py:164
  99.6 24.0 %copy-start.5 = (s32[3]{0:T(128)S(1)}, s32[3]{0:T(128)}, u32[]{:S(2)}) copy-start(s32[3]{0:T(128)} %constant.451) | copy-start | bytes 40
  642.1 11.0 %collective-permute-start.1 = (f32[5,1,16384]{2,0,1:T(8,128)S(1)}, f32[5,1,16384]{2,0,1:T(8,128)S(1)}, u32[]{:S(2)}, u32[]{:S(2)}) collective-permute-start(f32[5,1,16384]{2,0,1:T(8,128)S(1)} %get-tuple-element.606), channel_id=1, source_target_pairs={{8,0},{16,8},{24,16},{32,24},{40,32},{48,40},{56,48},{64,56},{72,6... | collective-permute-start | bytes 983048 | tf_op jit(solution)/shard_map/ppermute | solution.py:29
  646.5 14.2 %collective-permute-start.2 = (f32[5,1,16384]{2,0,1:T(8,128)S(1)}, f32[5,1,16384]{2,0,1:T(8,128)S(1)}, u32[]{:S(2)}, u32[]{:S(2)}) collective-permute-start(f32[5,1,16384]{2,0,1:T(8,128)S(1)} %get-tuple-element.605), channel_id=1, source_target_pairs={{0,8},{8,16},{16,24},{24,32},{32,40},{40,48},{48,56},{56,64},{64,7... | collective-permute-start | bytes 983048 | tf_op jit(solution)/shard_map/ppermute | solution.py:27
  661.6 7.7 collective-permute-start.3
  666.4 7.1 collective-permute-start.4
  691.1 8.6 %collective-permute-start.5 = (f32[5,1,16384]{2,0,1:T(8,128)S(1)}, f32[5,1,16384]{2,0,1:T(8,128)S(1)}, u32[]{:S(2)}, u32[]{:S(2)}) collective-permute-start(f32[5,1,16384]{2,0,1:T(8,128)S(1)} %get-tuple-element.604), channel_id=1, source_target_pairs={{8,0},{16,8},{24,16},{32,24},{40,32},{48,40},{56,48},{64,56},{72,6... | collective-permute-start | bytes 983048 | tf_op jit(solution)/shard_map/ppermute | solution.py:29
  693.0 14.2 %collective-permute-start.6 = (f32[5,1,16384]{2,0,1:T(8,128)S(1)}, f32[5,1,16384]{2,0,1:T(8,128)S(1)}, u32[]{:S(2)}, u32[]{:S(2)}) collective-permute-start(f32[5,1,16384]{2,0,1:T(8,128)S(1)} %get-tuple-element.603), channel_id=1, source_target_pairs={{0,8},{8,16},{16,24},{24,32},{32,40},{40,48},{48,56},{56,64},{64,7... | collective-permute-start | bytes 983048 | tf_op jit(solution)/shard_map/ppermute | solution.py:27
  707.3 6.2 collective-permute-start.7
  710.4 7.1 collective-permute-start.8
  728.7 14.2 %collective-permute-start.10 = (f32[5,1,16384]{2,0,1:T(8,128)S(1)}, f32[5,1,16384]{2,0,1:T(8,128)S(1)}, u32[]{:S(2)}, u32[]{:S(2)}) collective-permute-start(f32[5,1,16384]{2,0,1:T(8,128)S(1)} %get-tuple-element.601), channel_id=1, source_target_pairs={{0,8},{8,16},{16,24},{24,32},{32,40},{40,48},{48,56},{56,64},{64,7... | collective-permute-start | bytes 983048 | tf_op jit(solution)/shard_map/ppermute | solution.py:27
  730.6 14.0 %collective-permute-start.9 = (f32[5,1,16384]{2,0,1:T(8,128)S(1)}, f32[5,1,16384]{2,0,1:T(8,128)S(1)}, u32[]{:S(2)}, u32[]{:S(2)}) collective-permute-start(f32[5,1,16384]{2,0,1:T(8,128)S(1)} %get-tuple-element.602), channel_id=1, source_target_pairs={{8,0},{16,8},{24,16},{32,24},{40,32},{48,40},{56,48},{64,56},{72,6... | collective-permute-start | bytes 983048 | tf_op jit(solution)/shard_map/ppermute | solution.py:29
  744.7 6.2 collective-permute-start.11
  748.6 7.1 collective-permute-start.12
  772.1 7.3 collective-permute-start
  784.4 7.4 collective-permute-start
  796.8 7.4 collective-permute-start
  809.2 7.4 collective-permute-start
  821.5 7.4 collective-permute-start
  833.9 7.4 collective-permute-start
  846.3 7.4 collective-permute-start
  858.7 0.6 copy-start.2
  858.7 0.6 copy-start.3
where the time goes:
time: 872 us; the launch traced here: 859 us
  other arithmetic  422 us (48%)
  local copies, waits for them, and re-layouts  277 us (32%)
  waiting for transfers between devices  76.8 us (9%)
  starting transfers between devices  54.1 us (6%)
  blocking collectives  27 us (3%)
    scatter x128, other arithmetic  291 us
    scatter x192, local copies, waits for them, and re-layouts  198 us
    add x3, other arithmetic, on_device(): field = field + diffusion * (beside - 4.0 * field)  39.5 us
    reduce_sum x8, other arithmetic, particle_rates(): jnp.sum(steep * along * curl[component], axis=1)  39.1 us
    ppermute x8, waiting for transfers between devices, from_behind(): lax.ppermute(value, axis, [(i, (i + by) % count) for i in range(count)])  38.3 us
    ppermute x6, waiting for transfers between devices, extended(): lax.ppermute(tail, axis, [(i, (i + 1) % count) for i in range(ends)])  28.1 us
    scatter x1, local copies, waits for them, and re-layouts, on_device(): flow.at[1:4, :, ::stride].set(node_velocity.reshape(3, rows, NODE_Z))  27.6 us
    unnamed x21, local copies, waits for them, and re-layouts  27.3 us
  transfers between devices with their start and end apart: 22, of which 18 were waited for; matrix products, arithmetic and copies ran while one was open for 73% of the time, Pallas kernels for 0%

commit v1 on v0

--- a/solution.py
+++ b/solution.py
@@ -117,7 +117,8 @@
     target_slots = lax.axis_index("grid") * target_count + jnp.arange(target_count, dtype=jnp.int32)
     target_live = target_slots < shed_counts[wake_index]
     share = jnp.concatenate([particle_position, particle_strength, particle_core[None, :]], axis=0)
-    block = lax.all_gather(share, "grid", axis=1, tiled=True)
+    built = lax.all_to_all(jnp.stack([share for _ in range(lax.axis_size("grid"))]), "grid", 0, 0)
+    block = jnp.concatenate(built, axis=1)
 
     def visit(source, number, totals):
         source_live = slots < shed_counts[number]

time: 872 us -> 845 us (0.969)
  blocking collectives: 27 us -> 0 us
    all_gather x1 -> x0, blocking collectives: 27 us -> none  [on_device(): block = lax.all_gather(share, 'grid', axis=1, tiled=True)]
  transfers between devices with their start and end apart: 22 -> 23, of which waited for: 18 -> 21; matrix products, arithmetic and copies ran while one was open for 73% -> 5% of each run, Pallas kernels for 0% -> 0%
where the time goes in v1:
time: 845 us; the launch traced here: 833 us
  other arithmetic  421 us (50%)
  local copies, waits for them, and re-layouts  269 us (32%)
  waiting for transfers between devices  83.9 us (10%)
  starting transfers between devices  56.7 us (7%)
    scatter x128, other arithmetic  291 us
    scatter x192, local copies, waits for them, and re-layouts  198 us
    add x3, other arithmetic, on_device(): field = field + diffusion * (beside - 4.0 * field)  39.5 us
    reduce_sum x8, other arithmetic, particle_rates(): jnp.sum(steep * along * curl[component], axis=1)  39.1 us
    ppermute x8, waiting for transfers between devices, from_behind(): lax.ppermute(value, axis, [(i, (i + by) % count) for i in range(count)])  38.4 us
    scatter x1, local copies, waits for them, and re-layouts, on_device(): flow.at[1:4, :, ::stride].set(node_velocity.reshape(3, rows, NODE_Z))  27.6 us
    unnamed x21, local copies, waits for them, and re-layouts  27.3 us
    ppermute x6, waiting for transfers between devices, extended(): lax.ppermute(tail, axis, [(i, (i + 1) % count) for i in range(ends)])  27 us
  transfers between devices with their start and end apart: 23, of which 21 were waited for; matrix products, arithmetic and copies ran while one was open for 5% of the time, Pallas kernels for 0%

profile of v1, /device:TPU:80, one launch (start us, length us, event | category | flops | bytes accessed | tf_op | source)
XLA Modules:
  0.0 832.8 jit_solution(18131838848933984130)
XLA Ops:
  13.0 7.3 all-to-all-start
  25.7 5.7 all-to-all-start.1
  35.5 33.8 %while.50 = (s32[]{:T(128)}, f32[8,3,256]{2,1,0:T(4,128)}, f32[8,3,256]{2,0,1:T(8,128)S(1)}, f32[7,2048]{1,0:T(8,128)S(1)}, f32[1,2048]{1,0:T(1,128)S(1)}, /*index=5*/s32[]{:T(128)}, s32[]{:T(128)}, s32[]{:T(128)}, s32[]{}, s32[]{}) while((s32[]{:T(128)}, f32[8,3,256]{2,1,0:T(4,128)}, f32[8,3,256]{2,0,1:T(8,128)S(1)}, ...), condition=%wide.region_8.9_spmd.clone, body=%wide.region_4.8_spmd.clone.sunk | while | flops 13110788 | bytes 179853 | solution.py:89
  69.3 5.6 all-to-all-start.2
  75.0 20.3 %copy.69 = f32[5,16,16384]{1,2,0:T(8,128)} copy(f32[5,16,16384]{2,1,0:T(8,128)} %param.13) | data formatting | bytes 10485760
  99.0 489.6 %while.49 = (s32[]{:T(128)}, f32[5,16,16384]{1,2,0:T(8,128)}, s32[64,2]{0,1:T(2,128)S(1)}, f32[64,3,16]{2,0,1:T(8,128)S(1)}, s32[]{:T(128)}, /*index=5*/s32[3]{0:T(128)S(1)}, s32[1]{0:T(128)}, s32[]{:T(128)}) while((s32[]{:T(128)}, f32[5,16,16384]{1,2,0:T(8,128)}, s32[64,2]{0,1:T(2,128)S(1)}, f32[64,3,16]{2,0,1:T(8,128)S(1)}, s32[]{:T(128)}, ...), condition=%wide.while_cond, body=%wide.while_body.sunk | while | flops 67 | bytes 1123 | solution.py:170
  588.6 27.6 %copy.76 = f32[5,16,16384]{2,0,1:T(8,128)} copy(f32[5,16,16384]{1,2,0:T(8,128)} %get-tuple-element.407) | data formatting | bytes 10485760 | tf_op jit(solution)/shard_map/scatter | solution.py:170
  628.5 7.5 collective-permute-done.2
  643.3 5.0 collective-permute-done.4
  648.2 17.5 %fusion.60 = f32[5,16,16384]{2,0,1:T(8,128)S(1)} fusion(f32[5,16,16384]{2,0,1:T(8,128)} %copy.76, f32[5,18,1]{2,0,1:T(8,128)S(1)} %collective-permute-done.4, f32[5,1,16384]{2,0,1:T(8,128)S(1)} %collective-permute-done.1, f32[5,1,16384]{2,0,1:T(8,128)S(1)} %collective-permute-done.2, f32[5,18,1]{2,0,1:T(8,128)S(1)} %collective-permute-done.3, ...), kind=kLoop, calls=%fused_computation.117 | loop fusion | flops 26214400 | bytes 11928332 | tf_op jit(solution)/shard_map/add | solution.py:177
  675.1 6.8 collective-permute-done.6
  691.1 11.1 %fusion.54 = f32[5,16,16384]{2,0,1:T(8,128)S(1)} fusion(f32[5,16,16384]{2,0,1:T(8,128)S(1)} %fusion.60, f32[5,18,1]{2,0,1:T(8,128)S(1)} %collective-permute-done.8, f32[5,1,16384]{2,0,1:T(8,128)S(1)} %collective-permute-done.5, f32[5,1,16384]{2,0,1:T(8,128)S(1)} %collective-permute-done.6, f32[5,18,1]{2,0,1:T(8,128)S(1)} %collective-permute-done.7, ...), kind=kLoop, calls=%fused_computation.103 | loop fusion | flops 26214400 | bytes 11928332 | tf_op jit(solution)/shard_map/add | solution.py:177
  704.2 7.3 collective-permute-start.9
  711.4 4.9 fusion.79
  724.5 4.8 collective-permute-done.12
  729.3 11.0 %fusion.48 = f32[5,16,16384]{2,0,1:T(8,128)S(1)} fusion(f32[5,16,16384]{2,0,1:T(8,128)S(1)} %fusion.54, f32[5,18,1]{2,0,1:T(8,128)S(1)} %collective-permute-done.12, f32[5,1,16384]{2,0,1:T(8,128)S(1)} %collective-permute-done.9, f32[5,1,16384]{2,0,1:T(8,128)S(1)} %collective-permute-done.10, f32[5,18,1]{2,0,1:T(8,128)S(1)} %collective-permute-done.11, ...), kind=kLoop, calls=%fused_computation.89 | loop fusion | flops 26214400 | bytes 11928332 | tf_op jit(solution)/shard_map/add | solution.py:177
  740.3 5.4 copy.77
  745.7 86.5 %while.51 = (s32[]{:T(128)}, f32[7,2048]{1,0:T(8,128)S(1)}, f32[3,256]{1,0:T(4,128)S(1)}, f32[3,256]{1,0:T(4,128)S(1)}, s32[]{:T(128)}, /*index=5*/s32[16]{0:T(1...) while((s32[]{:T(128)}, f32[7,2048]{1,0:T(8,128)S(1)}, ...), condition=%wide.region_29.30_spmd.clone, body=%wide.region_19.29_spmd.clone.sunk | while | flops 24654864 | bytes 581992 | solution.py:145
  747.5 5.5 collective-permute-done
  753.0 4.9 fusion.117
  759.9 5.5 collective-permute-done
  765.4 4.9 fusion.117
  772.3 5.5 collective-permute-done
  777.8 4.9 fusion.117
  784.6 5.5 collective-permute-done
  790.2 4.9 fusion.117
  797.0 5.5 collective-permute-done
  802.5 4.9 fusion.117
  809.4 5.5 collective-permute-done
  814.9 4.9 fusion.117
  821.7 5.5 collective-permute-done
  827.3 4.9 fusion.117
  (507 shorter events, 610.4 us)
Async XLA Ops:
  0.6 19.7 %copy-start = (s32[16,16384]{1,0:T(8,128)S(1)}, s32[16,16384]{1,0:T(8,128)}, u32[]{:S(2)}) copy-start(s32[16,16384]{1,0:T(8,128)} %param.14) | copy-start | bytes 3145732
  8.7 12.1 %copy-start.1 = (f32[3,256]{1,0:T(4,128)S(1)}, f32[3,256]{1,0:T(4,128)}, u32[]{:S(2)}) copy-start(f32[3,256]{1,0:T(4,128)} %param.17) | copy-start | bytes 9220
  8.7 12.1 %copy-start.4 = (f32[3,256]{1,0:T(4,128)S(1)}, f32[3,256]{1,0:T(4,128)}, u32[]{:S(2)}) copy-start(f32[3,256]{1,0:T(4,128)} %param.16) | copy-start | bytes 9220
  8.7 12.1 %copy-start.6 = (f32[256]{0:T(256)S(1)}, f32[256]{0:T(256)}, u32[]{:S(2)}) copy-start(f32[256]{0:T(256)} %param.18) | copy-start | bytes 3076
  8.7 22.7 %copy-start.8 = (f32[3,5]{1,0:T(4,128)S(1)}, f32[3,5]{1,0:T(4,128)}, u32[]{:S(2)}) copy-start(f32[3,5]{1,0:T(4,128)} %param.15) | copy-start | bytes 184
  8.7 22.7 %copy-start.7 = (s32[16]{0:T(128)S(1)}, s32[16]{0:T(128)}, u32[]{:S(2)}) copy-start(s32[16]{0:T(128)} %param.19) | copy-start | bytes 196
  13.0 12.1 %all-to-all-start = ((f32[3,16,128]{2,0,1:T(4,128)}), f32[3,16,128]{2,0,1:T(4,128)S(1)}, u32[]{:S(2)}, u32[]{:S(2)}) async-start(f32[3,16,128]{2,0,1:T(4,128)} %copy.62), calls=%async_computation | async-start | bytes 65536 | tf_op jit(solution)/shard_map/all_to_all | solution.py:157
  25.7 9.8 %all-to-all-start.1 = ((f32[8,7,256]{2,1,0:T(8,128)}), f32[8,7,256]{2,1,0:T(8,128)S(1)}, u32[]{:S(2)}, u32[]{:S(2)}) async-start(f32[8,7,256]{2,1,0:T(8,128)} %stack.131), calls=%async_computation.1 | async-start | bytes 131072 | tf_op jit(solution)/shard_map/all_to_all | solution.py:120
  69.3 26.0 %all-to-all-start.2 = ((f32[3,16,128]{2,0,1:T(4,128)}), f32[3,16,128]{2,0,1:T(4,128)S(1)}, u32[]{:S(2)}, u32[]{:S(2)}) async-start(f32[3,16,128]{2,0,1:T(4,128)} %bitcast.15), calls=%async_computation.2 | async-start | bytes 65536 | tf_op jit(solution)/shard_map/all_to_all | solution.py:165
  75.0 24.0 %copy-start.5 = (s32[3]{0:T(128)S(1)}, s32[3]{0:T(128)}, u32[]{:S(2)}) copy-start(s32[3]{0:T(128)} %constant.451) | copy-start | bytes 40
  617.5 11.0 %collective-permute-start.1 = (f32[5,1,16384]{2,0,1:T(8,128)S(1)}, f32[5,1,16384]{2,0,1:T(8,128)S(1)}, u32[]{:S(2)}, u32[]{:S(2)}) collective-permute-start(f32[5,1,16384]{2,0,1:T(8,128)S(1)} %get-tuple-element.606), channel_id=1, source_target_pairs={{8,0},{16,8},{24,16},{32,24},{40,32},{48,40},{56,48},{64,56},{72,6... | collective-permute-start | bytes 983048 | tf_op jit(solution)/shard_map/ppermute | solution.py:29
  621.8 14.2 %collective-permute-start.2 = (f32[5,1,16384]{2,0,1:T(8,128)S(1)}, f32[5,1,16384]{2,0,1:T(8,128)S(1)}, u32[]{:S(2)}, u32[]{:S(2)}) collective-permute-start(f32[5,1,16384]{2,0,1:T(8,128)S(1)} %get-tuple-element.605), channel_id=1, source_target_pairs={{0,8},{8,16},{16,24},{24,32},{32,40},{40,48},{48,56},{56,64},{64,7... | collective-permute-start | bytes 983048 | tf_op jit(solution)/shard_map/ppermute | solution.py:27
  637.0 6.2 collective-permute-start.3
  641.1 7.1 collective-permute-start.4
  665.8 9.3 %collective-permute-start.5 = (f32[5,1,16384]{2,0,1:T(8,128)S(1)}, f32[5,1,16384]{2,0,1:T(8,128)S(1)}, u32[]{:S(2)}, u32[]{:S(2)}) collective-permute-start(f32[5,1,16384]{2,0,1:T(8,128)S(1)} %get-tuple-element.604), channel_id=1, source_target_pairs={{8,0},{16,8},{24,16},{32,24},{40,32},{48,40},{56,48},{64,56},{72,6... | collective-permute-start | bytes 983048 | tf_op jit(solution)/shard_map/ppermute | solution.py:29
  667.7 14.2 %collective-permute-start.6 = (f32[5,1,16384]{2,0,1:T(8,128)S(1)}, f32[5,1,16384]{2,0,1:T(8,128)S(1)}, u32[]{:S(2)}, u32[]{:S(2)}) collective-permute-start(f32[5,1,16384]{2,0,1:T(8,128)S(1)} %get-tuple-element.603), channel_id=1, source_target_pairs={{0,8},{8,16},{16,24},{24,32},{32,40},{40,48},{48,56},{56,64},{64,7... | collective-permute-start | bytes 983048 | tf_op jit(solution)/shard_map/ppermute | solution.py:27
  670.7 17.3 %collective-permute-start.13 = (f32[7,2048]{1,0:T(8,128)S(1)}, f32[7,2048]{1,0:T(8,128)S(1)}, u32[]{:S(2)}, u32[]{:S(2)}) collective-permute-start(f32[7,2048]{1,0:T(8,128)S(1)} %get-tuple-element.951), channel_id=1, source_target_pairs={{0,104},{8,112},{16,120},{24,0},{32,8},{40,16},{48,24},{56,32},{64... | collective-permute-start | bytes 172040 | tf_op jit(solution)/shard_map/ppermute | solution.py:16
  682.0 6.2 collective-permute-start.7
  683.9 7.1 collective-permute-start.8
  702.2 14.2 %collective-permute-start.10 = (f32[5,1,16384]{2,0,1:T(8,128)S(1)}, f32[5,1,16384]{2,0,1:T(8,128)S(1)}, u32[]{:S(2)}, u32[]{:S(2)}) collective-permute-start(f32[5,1,16384]{2,0,1:T(8,128)S(1)} %get-tuple-element.601), channel_id=1, source_target_pairs={{0,8},{8,16},{16,24},{24,32},{32,40},{40,48},{48,56},{56,64},{64,7... | collective-permute-start | bytes 983048 | tf_op jit(solution)/shard_map/ppermute | solution.py:27
  704.2 14.0 %collective-permute-start.9 = (f32[5,1,16384]{2,0,1:T(8,128)S(1)}, f32[5,1,16384]{2,0,1:T(8,128)S(1)}, u32[]{:S(2)}, u32[]{:S(2)}) collective-permute-start(f32[5,1,16384]{2,0,1:T(8,128)S(1)} %get-tuple-element.602), channel_id=1, source_target_pairs={{8,0},{16,8},{24,16},{32,24},{40,32},{48,40},{56,48},{64,56},{72,6... | collective-permute-start | bytes 983048 | tf_op jit(solution)/shard_map/ppermute | solution.py:29
  718.2 6.2 collective-permute-start.11
  722.1 7.1 collective-permute-start.12
  745.7 7.3 collective-permute-start
  758.0 7.4 collective-permute-start
  770.4 7.4 collective-permute-start
  782.7 7.4 collective-permute-start
  795.1 7.4 collective-permute-start
  807.5 7.4 collective-permute-start
  819.9 7.4 collective-permute-start
  832.2 0.6 copy-start.2
  832.2 0.6 copy-start.3
